TPU v7x, 32 devices: a whole 2x2x4 slice. The times are simulated.
32 devices in a mesh: dp: 8 (over z, x), seq: 4 (over y, core).
Axes of the slice: x: 2, y: 2, z: 4, core: 2. Of those that a mesh axis runs over, the one named last changes fastest.
Arguments:
- tokens: float32 [16, 256, 1024], P('dp', 'seq'), may hold values from -6 to 6
- output_cotangent: float32 [16, 256, 1024], P('dp', 'seq'), may hold values from -0.5 to 0.5
- placement: int32 [8], replicated, may hold values from 0 to 15, as said below
- inward: float32 [1024, 3072], P(('dp', 'seq'))
- outward: float32 [1024, 1024], P(('dp', 'seq')), may hold values from -0.75 to 0.75
- attend_vectors: float32 [5, 1024], P(None, ('dp', 'seq'))
- expand: float32 [1024, 4096], P(('dp', 'seq')), may hold values from -0.1875 to 0.1875
- shrink: float32 [4096, 1024], P(('dp', 'seq')), may hold values from -0.09375 to 0.09375
- feed_vectors: float32 [3, 1024], P(None, ('dp', 'seq'))
- expand_bias: float32 [4096], P(('dp', 'seq')), may hold values from -3 to 3
- inward_moments: float32 [2, 1024, 3072], P(None, ('dp', 'seq')), as said below
- outward_moments: float32 [2, 1024, 1024], P(None, ('dp', 'seq'))
- attend_moments: float32 [2, 5, 1024], P(None, None, ('dp', 'seq'))
- expand_moments: float32 [2, 1024, 4096], P(None, ('dp', 'seq'))
- shrink_moments: float32 [2, 4096, 1024], P(None, ('dp', 'seq'))
- feed_moments: float32 [2, 3, 1024], P(None, None, ('dp', 'seq'))
- bias_moments: float32 [2, 4096], P(None, ('dp', 'seq'))
Outputs:
- block_output: float32 [16, 256, 1024], P('dp', 'seq')
- input_gradient: float32 [16, 256, 1024], P('dp', 'seq')
- inward_gradient: float32 [1024, 3072], P(('dp', 'seq'))
- outward_gradient: float32 [1024, 1024], P(('dp', 'seq'))
- attend_gradient: float32 [5, 1024], P(None, ('dp', 'seq'))
- expand_gradient: float32 [1024, 4096], P(('dp', 'seq'))
- shrink_gradient: float32 [4096, 1024], P(('dp', 'seq'))
- feed_gradient: float32 [3, 1024], P(None, ('dp', 'seq'))
- bias_gradient: float32 [4096], P(('dp', 'seq'))
- inward_new: float32 [1024, 3072], P(('dp', 'seq'))
- outward_new: float32 [1024, 1024], P(('dp', 'seq'))
- attend_new: float32 [5, 1024], P(None, ('dp', 'seq'))
- expand_new: float32 [1024, 4096], P(('dp', 'seq'))
- shrink_new: float32 [4096, 1024], P(('dp', 'seq'))
- feed_new: float32 [3, 1024], P(None, ('dp', 'seq'))
- bias_new: float32 [4096], P(('dp', 'seq'))
- inward_state: float32 [2, 1024, 3072], P(None, ('dp', 'seq'))
- outward_state: float32 [2, 1024, 1024], P(None, ('dp', 'seq'))
- attend_state: float32 [2, 5, 1024], P(None, None, ('dp', 'seq'))
- expand_state: float32 [2, 1024, 4096], P(None, ('dp', 'seq'))
- shrink_state: float32 [2, 4096, 1024], P(None, ('dp', 'seq'))
- feed_state: float32 [2, 3, 1024], P(None, None, ('dp', 'seq'))
- bias_state: float32 [2, 4096], P(None, ('dp', 'seq'))
Inputs may be any that keep to these rules, and one draw needn't show every extreme that they name: `placement`: entries are distinct slot numbers; slot s belongs to index s // 2 of dp; in every draw some index of dp holds 2 sequences. `inward_moments`: the second moment (index 1) is positive.
All inputs are finite; a program needn't handle non-finite values.
Results may differ from a plain program's by a relative error of at most 0.012.
Values may be sent and summed in bfloat16 or wider, within the bound.
A program may use at most 192 MiB of HBM per device.

v0:
```python
import math
import jax
import jax.numpy as jnp
from jax import lax
from jax.sharding import PartitionSpec as P

HEADS = 16
HEAD_DIM = 64
norm_epsilon = 1e-05
beta_first = 0.9
beta_second = 0.95
adam_epsilon = 1e-08
learn_rate = 0.01
weight_decay = 0.1
adam_steps = 4
gelu_scale = 0.7978845608028654
gelu_cubic = 0.044715
masked_score = -1e30


def halved(operand):
    return operand.astype(jnp.bfloat16)


def normalize(operand):
    average = jnp.mean(operand, axis=-1, keepdims=True)
    centered = operand - average
    variance = jnp.mean(centered * centered, axis=-1, keepdims=True)
    inverse = lax.rsqrt(variance + norm_epsilon)
    return (centered * inverse, inverse)


def norm_back(upstream, normed, inverse):
    first_mean = jnp.mean(upstream, axis=-1, keepdims=True)
    second_mean = jnp.mean(upstream * normed, axis=-1, keepdims=True)
    return inverse * (upstream - first_mean - normed * second_mean)


def gelu_pair(upper):
    inner_arg = gelu_scale * (upper + gelu_cubic * upper * upper * upper)
    tangent = jnp.tanh(inner_arg)
    active = 0.5 * upper * (1.0 + tangent)
    slope = 0.5 * (1.0 + tangent) + 0.5 * upper * (1.0 - tangent * tangent) * gelu_scale * (
        1.0 + 3.0 * gelu_cubic * upper * upper
    )
    return (active, slope)


def adamw_update(parameter, gradient, moments, decay_rate):
    first_moment = beta_first * moments[0] + (1.0 - beta_first) * gradient
    second = beta_second * moments[1] + (1.0 - beta_second) * gradient * gradient
    unbiased_first = first_moment / (1.0 - beta_first**adam_steps)
    unbiased_second = second / (1.0 - beta_second**adam_steps)
    update = unbiased_first / (jnp.sqrt(unbiased_second) + adam_epsilon) + decay_rate * parameter
    return (parameter - learn_rate * update, jnp.stack([first_moment, second]))


def spread_columns(piece, groups, inner):
    rows = piece.shape[0]
    parts = piece.reshape(rows, -1, groups, inner)
    moved = lax.all_to_all(parts, "seq", 2, 0, tiled=True)
    return moved.reshape(groups * rows, -1)


def collect_columns(piece, groups, inner):
    rows = piece.shape[0] // groups
    parts = piece.reshape(rows * groups, -1, 1, inner)
    moved = lax.all_to_all(parts, "seq", 0, 2, tiled=True)
    return moved.reshape(rows, -1)


def body(
    tokens,
    output_cotangent,
    placement,
    inward,
    outward,
    attend_vectors,
    expand,
    shrink,
    feed_vectors,
    expand_bias,
    inward_moments,
    outward_moments,
    attend_moments,
    expand_moments,
    shrink_moments,
    feed_moments,
    bias_moments,
):
    slot_count, block_size, model_width = tokens.shape
    groups = lax.axis_size("seq")
    replicas = lax.axis_size("dp")
    devices = groups * replicas
    mine = lax.axis_index("seq")
    length = block_size * groups
    row_count = slot_count * block_size
    all_rows = slot_count * length
    head_count = HEADS // groups
    part_width = head_count * HEAD_DIM
    vec_width = attend_vectors.shape[1]
    hidden_part = expand_bias.shape[0]
    score_scale = 1.0 / math.sqrt(HEAD_DIM)
    whole = ("dp", "seq")

    def gather_rows(local):
        full = lax.all_gather(local.reshape(slot_count, block_size, -1), "seq", axis=1, tiled=True)
        return full.reshape(all_rows, -1)

    def scatter_rows(partial):
        own = lax.psum_scatter(
            halved(partial).reshape(slot_count, length, -1), "seq", scatter_dimension=1, tiled=True
        )
        return own.reshape(row_count, -1).astype(jnp.float32)

    slot_ids = lax.axis_index("dp") * slot_count + jnp.arange(slot_count, dtype=jnp.int32)
    live_mask = jnp.any(placement[None, :] == slot_ids[:, None], axis=1).astype(jnp.float32)[
        :, None, None
    ]
    small = jnp.concatenate(
        [halved(attend_vectors).reshape(-1), halved(feed_vectors).reshape(-1), halved(expand_bias)]
    )
    small_rows = 16
    small_block = jnp.pad(small, (0, small_rows * model_width - small.shape[0])).reshape(
        small_rows, model_width
    )
    out_rows = outward.shape[0]
    first = lax.all_gather(
        jnp.concatenate([halved(outward), small_block], axis=0), whole, axis=0, tiled=True
    ).reshape(devices, out_rows + small_rows, model_width)
    out_whole = first[:, :out_rows].reshape(devices * out_rows, model_width)
    small_all = first[:, out_rows:].reshape(devices, -1)[:, : small.shape[0]].astype(jnp.float32)
    vectors = jnp.transpose(
        small_all[:, : 8 * vec_width].reshape(devices, 8, vec_width), (1, 0, 2)
    ).reshape(8, model_width)
    vec_one = vectors[:5]
    vec_two = vectors[5:]
    bias_all = small_all[:, 8 * vec_width :].reshape(replicas, groups, hidden_part)
    bias_part = lax.dynamic_index_in_dim(bias_all, mine, 1, keepdims=False).reshape(-1)
    in_width = 3 * part_width
    moved_in = spread_columns(halved(inward), groups, part_width)
    moved_up = spread_columns(halved(expand), groups, hidden_part)
    in_part = lax.all_gather(moved_in, "dp", axis=0, tiled=True)
    up_part = lax.all_gather(moved_up, "dp", axis=0, tiled=True)
    down_part = lax.all_gather(halved(shrink), "dp", axis=0, tiled=True)
    cotangent = (output_cotangent * live_mask).reshape(row_count, model_width)
    cot_all = gather_rows(halved(cotangent))
    feed_bias_grad = jnp.sum(cotangent, axis=0)
    flat_tokens = tokens.reshape(row_count, model_width)
    normed_one, inverse_one = normalize(flat_tokens)
    lifted_one = gather_rows(halved(normed_one * vec_one[0] + vec_one[1]))
    packed = jnp.dot(lifted_one, in_part, preferred_element_type=jnp.float32)
    bias_query = lax.dynamic_slice_in_dim(vec_one[2], mine * part_width, part_width)
    bias_value = lax.dynamic_slice_in_dim(vec_one[3], mine * part_width, part_width)

    def to_heads(operand):
        return jnp.transpose(
            operand.reshape(slot_count, length, head_count, HEAD_DIM), (0, 2, 1, 3)
        )

    def from_heads(operand):
        return jnp.transpose(operand, (0, 2, 1, 3)).reshape(all_rows, part_width)

    queries = to_heads(halved(packed[:, :part_width] + bias_query))
    keys = to_heads(halved(packed[:, part_width : 2 * part_width]))
    values = to_heads(halved(packed[:, 2 * part_width :] + bias_value))
    positions = jnp.arange(length)
    allowed = positions[None, :] <= positions[:, None]
    scores = (
        jnp.einsum("shqd,shkd->shqk", queries, keys, preferred_element_type=jnp.float32)
        * score_scale
    )
    scores = jnp.where(allowed, scores, masked_score)
    score_peak = jnp.max(scores, axis=-1, keepdims=True)
    log_total = score_peak + jnp.log(jnp.sum(jnp.exp(scores - score_peak), axis=-1, keepdims=True))
    weights_full = jnp.exp(scores - log_total)
    weights_half = halved(weights_full)
    attended_heads = halved(
        jnp.einsum("shqk,shkd->shqd", weights_half, values, preferred_element_type=jnp.float32)
    )
    attended = lax.all_to_all(
        from_heads(attended_heads).reshape(slot_count, length, part_width), "seq", 1, 2, tiled=True
    ).reshape(row_count, model_width)
    projected = jnp.dot(attended, out_whole, preferred_element_type=jnp.float32)
    middle = flat_tokens + projected + vec_one[4]
    normed_two, inverse_two = normalize(middle)
    lifted_two = gather_rows(halved(normed_two * vec_two[0] + vec_two[1]))
    upper = jnp.dot(lifted_two, up_part, preferred_element_type=jnp.float32) + bias_part
    active_full, slope = gelu_pair(upper)
    active = halved(active_full)
    upper_grad = (
        lax.dot_general(
            cot_all, down_part, (((1,), (1,)), ((), ())), preferred_element_type=jnp.float32
        )
        * slope
    )
    upper_half = halved(upper_grad)
    lift_two_grad = scatter_rows(
        lax.dot_general(
            upper_half, up_part, (((1,), (1,)), ((), ())), preferred_element_type=jnp.float32
        )
    )
    fed = scatter_rows(jnp.dot(active, down_part, preferred_element_type=jnp.float32))
    block_output = (middle + fed + vec_two[2]).reshape(
        slot_count, block_size, model_width
    ) * live_mask

    def outer(left, right):
        return halved(
            lax.dot_general(
                left, right, (((0,), (0,)), ((), ())), preferred_element_type=jnp.float32
            )
        )

    shrink_sum = lax.psum_scatter(
        outer(active, cot_all), "dp", scatter_dimension=0, tiled=True
    ).astype(jnp.float32)
    expand_sum = collect_columns(
        lax.psum_scatter(outer(lifted_two, upper_half), "dp", scatter_dimension=0, tiled=True),
        groups,
        hidden_part,
    ).astype(jnp.float32)
    bias_grad = jnp.sum(upper_grad, axis=0).reshape(replicas, 1, hidden_part)
    gain_two_grad = jnp.sum(lift_two_grad * normed_two, axis=0)
    shift_two_grad = jnp.sum(lift_two_grad, axis=0)
    middle_grad = cotangent + norm_back(lift_two_grad * vec_two[0], normed_two, inverse_two)
    middle_half = halved(middle_grad)
    out_bias_grad = jnp.sum(middle_grad, axis=0)
    attended_back = halved(
        lax.dot_general(
            middle_half, out_whole, (((1,), (1,)), ((), ())), preferred_element_type=jnp.float32
        )
    )
    attended_grad = to_heads(
        lax.all_to_all(
            attended_back.reshape(slot_count, block_size, model_width), "seq", 2, 1, tiled=True
        ).reshape(all_rows, part_width)
    )
    outward_sum = lax.psum_scatter(
        outer(attended, middle_half), whole, scatter_dimension=0, tiled=True
    ).astype(jnp.float32)
    delta_sum = jnp.sum(
        attended_grad.astype(jnp.float32) * attended_heads.astype(jnp.float32),
        axis=-1,
        keepdims=True,
    )
    weight_grad = jnp.einsum(
        "shqd,shkd->shqk", attended_grad, values, preferred_element_type=jnp.float32
    )
    score_grad = halved(weights_full * (weight_grad - delta_sum) * score_scale)
    query_grad = from_heads(
        jnp.einsum("shqk,shkd->shqd", score_grad, keys, preferred_element_type=jnp.float32)
    )
    key_grad = from_heads(
        jnp.einsum("shqk,shqd->shkd", score_grad, queries, preferred_element_type=jnp.float32)
    )
    value_grad = from_heads(
        jnp.einsum(
            "shqk,shqd->shkd", weights_half, attended_grad, preferred_element_type=jnp.float32
        )
    )
    packed_grad = halved(jnp.concatenate([query_grad, key_grad, value_grad], axis=1))
    lift_one_grad = scatter_rows(
        lax.dot_general(
            packed_grad, in_part, (((1,), (1,)), ((), ())), preferred_element_type=jnp.float32
        )
    )
    inward_sum = collect_columns(
        lax.psum_scatter(outer(lifted_one, packed_grad), "dp", scatter_dimension=0, tiled=True),
        groups,
        part_width,
    ).astype(jnp.float32)

    def place_part(part):
        return lax.dynamic_update_slice_in_dim(
            jnp.zeros((model_width,), jnp.float32), part, mine * part_width, 0
        )

    gain_one_grad = jnp.sum(lift_one_grad * normed_one, axis=0)
    shift_one_grad = jnp.sum(lift_one_grad, axis=0)
    tokens_grad = middle_grad + norm_back(lift_one_grad * vec_one[0], normed_one, inverse_one)
    input_gradient = tokens_grad.reshape(slot_count, block_size, model_width) * live_mask
    vector_grads = jnp.stack(
        [
            gain_one_grad,
            shift_one_grad,
            place_part(jnp.sum(query_grad, axis=0)),
            place_part(jnp.sum(value_grad, axis=0)),
            out_bias_grad,
            gain_two_grad,
            shift_two_grad,
            feed_bias_grad,
        ]
    ).T
    bias_placed = lax.dynamic_update_slice_in_dim(
        jnp.zeros((replicas, groups, hidden_part), jnp.float32), bias_grad, mine, 1
    ).reshape(model_width, -1)
    small_sum = lax.psum_scatter(
        jnp.concatenate([vector_grads, bias_placed], axis=1), whole, scatter_dimension=0, tiled=True
    )
    attend_vec_sum = small_sum[:, :5].T
    feed_vec_sum = small_sum[:, 5:8].T
    bias_sum = small_sum[:, 8:].reshape(-1)
    inward_new, inward_state = adamw_update(inward, inward_sum, inward_moments, weight_decay)
    outward_new, outward_state = adamw_update(outward, outward_sum, outward_moments, weight_decay)
    attend_new, attend_state = adamw_update(attend_vectors, attend_vec_sum, attend_moments, 0.0)
    expand_new, expand_state = adamw_update(expand, expand_sum, expand_moments, weight_decay)
    shrink_new, shrink_state = adamw_update(shrink, shrink_sum, shrink_moments, weight_decay)
    feed_new, feed_state = adamw_update(feed_vectors, feed_vec_sum, feed_moments, 0.0)
    bias_new, bias_state = adamw_update(expand_bias, bias_sum, bias_moments, 0.0)
    return (
        block_output,
        input_gradient,
        inward_sum,
        outward_sum,
        attend_vec_sum,
        expand_sum,
        shrink_sum,
        feed_vec_sum,
        bias_sum,
        inward_new,
        outward_new,
        attend_new,
        expand_new,
        shrink_new,
        feed_new,
        bias_new,
        inward_state,
        outward_state,
        attend_state,
        expand_state,
        shrink_state,
        feed_state,
        bias_state,
    )


def solution(mesh):
    placed = (
        P("dp", "seq", None),
        P("dp", "seq", None),
        P(),
        P(("dp", "seq"), None),
        P(("dp", "seq"), None),
        P(None, ("dp", "seq")),
        P(("dp", "seq"), None),
        P(("dp", "seq"), None),
        P(None, ("dp", "seq")),
        P(("dp", "seq")),
        P(None, ("dp", "seq"), None),
        P(None, ("dp", "seq"), None),
        P(None, None, ("dp", "seq")),
        P(None, ("dp", "seq"), None),
        P(None, ("dp", "seq"), None),
        P(None, None, ("dp", "seq")),
        P(None, ("dp", "seq")),
    )
    return jax.shard_map(
        body,
        mesh=mesh,
        in_specs=placed,
        out_specs=(
            P("dp", "seq", None),
            P("dp", "seq", None),
            P(("dp", "seq"), None),
            P(("dp", "seq"), None),
            P(None, ("dp", "seq")),
            P(("dp", "seq"), None),
            P(("dp", "seq"), None),
            P(None, ("dp", "seq")),
            P(("dp", "seq")),
            P(("dp", "seq"), None),
            P(("dp", "seq"), None),
            P(None, ("dp", "seq")),
            P(("dp", "seq"), None),
            P(("dp", "seq"), None),
            P(None, ("dp", "seq")),
            P(("dp", "seq")),
            P(None, ("dp", "seq"), None),
            P(None, ("dp", "seq"), None),
            P(None, None, ("dp", "seq")),
            P(None, ("dp", "seq"), None),
            P(None, ("dp", "seq"), None),
            P(None, None, ("dp", "seq")),
            P(None, ("dp", "seq")),
        ),
        check_vma=False,
    )
```

profile of v0, /device:TPU:0, one launch (start us, length us, event | category | flops | bytes accessed | tf_op | source)
XLA Modules:
  0.0 881.6 jit_solution(11967319726546057766)
XLA Ops:
  12.4 9.4 %all_to_all.78 = bf16[32,3,4,256]{3,0,1,2:T(8,128)(2,1)S(1)} all-to-all(bf16[32,3,4,256]{3,0,1,2:T(8,128)(2,1)S(1)} %copy.236), channel_id=1, replica_groups=mesh['dp'=8,'seq'=4] {'seq'}, dimensions={2} | all-to-all | bytes 393216 | tf_op jit(solution)/shard_map/all_to_all | solution.py:61
  23.1 50.3 %all-gather.8.cloned.1.call-done = bf16[1536,1024]{1,0:T(8,128)(2,1)} async-done(((bf16[48,1024]{1,0:T(8,128)(2,1)}), bf16[1536,1024]{1,0:T(8,128)(2,1)}) %all-gather.8.cloned.1.call-update) | async-done | bytes 3145744 | tf_op jit(solution)/shard_map/all_gather | solution.py:128
  77.6 8.5 all_to_all.79
  87.3 31.8 %all-gather.12.cloned.1.call-done = bf16[1024,768]{1,0:T(8,128)(2,1)} async-done(((bf16[128,768]{1,0:T(8,128)(2,1)}), bf16[1024,768]{1,0:T(8,128)(2,1)}) %all-gather.12.cloned.1.call-update) | async-done | bytes 1572880 | tf_op jit(solution)/shard_map/all_gather | solution.py:143
  119.1 17.2 %all-gather.10.cloned.1.call-done = bf16[2,256,1024]{2,1,0:T(8,128)(2,1)} async-done(((bf16[2,64,1024]{2,1,0:T(8,128)(2,1)}), bf16[2,256,1024]{2,1,0:T(8,128)(2,1)}) %all-gather.10.cloned.1.call-update) | async-done | bytes 1048592 | tf_op jit(solution)/shard_map/all_gather | solution.py:107
  136.3 2.7 fusion.89
  142.3 3.4 all-to-all-start.1
  145.8 3.3 slice.165
  158.5 29.5 %all-gather.16.cloned.1.call-done = bf16[1024,1024]{1,0:T(8,128)(2,1)} async-done(((bf16[128,1024]{1,0:T(8,128)(2,1)}), bf16[1024,1024]{1,0:T(8,128)(2,1)}) %all-gather.16.cloned.1.call-update) | async-done | bytes 2097168 | tf_op jit(solution)/shard_map/all_gather | solution.py:144
  188.0 17.3 %all-gather.14.cloned.1.call-done = bf16[2,256,1024]{2,1,0:T(8,128)(2,1)} async-done(((bf16[2,64,1024]{2,1,0:T(8,128)(2,1)}), bf16[2,256,1024]{2,1,0:T(8,128)(2,1)}) %all-gather.14.cloned.1.call-update) | async-done | bytes 1048592 | tf_op jit(solution)/shard_map/all_gather | solution.py:107
  205.3 4.5 fusion.90
  209.8 14.2 %all-gather.20.cloned.1.call-done = bf16[2,256,1024]{2,1,0:T(8,128)(2,1)} async-done(((bf16[2,64,1024]{2,1,0:T(8,128)(2,1)}), bf16[2,256,1024]{2,1,0:T(8,128)(2,1)}) %all-gather.20.cloned.1.call-update) | async-done | bytes 1048592 | tf_op jit(solution)/shard_map/all_gather | solution.py:107
  224.0 4.9 convolution_convert_fusion
  229.0 68.5 %reduce-scatter.23.cloned.1.call-done = bf16[128,1024]{1,0:T(8,128)(2,1)} async-done(((bf16[1024,1024]{1,0:T(8,128)(2,1)}), bf16[128,1024]{1,0:T(8,128)(2,1)}) %reduce-scatter.23.cloned.1.call-update) | async-done | bytes 262160 | tf_op jit(solution)/shard_map/reduce_scatter | solution.py:215
  301.4 48.0 %all-gather.18.cloned.1.call-done = bf16[1024,1024]{1,0:T(8,128)(2,1)} async-done(((bf16[128,1024]{1,0:T(8,128)(2,1)}), bf16[1024,1024]{1,0:T(8,128)(2,1)}) %all-gather.18.cloned.1.call-update) | async-done | bytes 2097168 | tf_op jit(solution)/shard_map/all_gather | solution.py:145
  349.4 5.1 fusion.88
  356.9 4.7 convolution_convert_fusion.6
  361.7 18.6 %reduce-scatter.13.cloned.1.call-done = bf16[2,64,1024]{2,1,0:T(8,128)(2,1)} async-done(((bf16[2,256,1024]{2,1,0:T(8,128)(2,1)}), bf16[2,64,1024]{2,1,0:T(8,128)(2,1)}) %reduce-scatter.13.cloned.1.call-update) | async-done | bytes 262160 | tf_op jit(solution)/shard_map/reduce_scatter | solution.py:111
  382.7 25.3 %reduce-scatter.11.cloned.1.call-done = bf16[2,64,1024]{2,1,0:T(8,128)(2,1)} async-done(((bf16[2,256,1024]{2,1,0:T(8,128)(2,1)}), bf16[2,64,1024]{2,1,0:T(8,128)(2,1)}) %reduce-scatter.11.cloned.1.call-update) | async-done | bytes 262160 | tf_op jit(solution)/shard_map/reduce_scatter | solution.py:111
  408.0 2.4 fusion.81
  413.8 9.1 %all_to_all.80 = bf16[4,2,16384]{2,1,0:T(2,128)(2,1)} all-to-all(bf16[4,2,16384]{2,1,0:T(2,128)(2,1)S(1)} %reshape.573), channel_id=1, replica_groups=mesh['dp'=8,'seq'=4] {'seq'}, dimensions={0} | all-to-all | bytes 524288 | tf_op jit(solution)/shard_map/all_to_all | solution.py:235
  435.1 2.6 convolution_convert_fusion.1
  438.8 21.0 %reduce-scatter.15.cloned.1.call-done = bf16[2,64,1024]{2,1,0:T(8,128)(2,1)} async-done(((bf16[2,256,1024]{2,1,0:T(8,128)(2,1)}), bf16[2,64,1024]{2,1,0:T(8,128)(2,1)}) %reduce-scatter.15.cloned.1.call-update) | async-done | bytes 262160 | tf_op jit(solution)/shard_map/reduce_scatter | solution.py:111
  462.2 3.5 convolution_convert_fusion.3
  469.2 62.3 %reduce-scatter.21.cloned.1.call-done = bf16[128,1024]{1,0:T(8,128)(2,1)} async-done(((bf16[1024,1024]{1,0:T(8,128)(2,1)}), bf16[128,1024]{1,0:T(8,128)(2,1)}) %reduce-scatter.21.cloned.1.call-update) | async-done | bytes 262160 | tf_op jit(solution)/shard_map/reduce_scatter | solution.py:219
  533.1 3.4 all-to-all-start.5
  538.1 4.5 all-to-all-done.5
  545.9 122.6 %reduce-scatter.25.cloned.1.call-done = f32[32,12]{1,0:T(8,128)} async-done(((f32[1024,12]{1,0:T(8,128)}), f32[32,12]{1,0:T(8,128)}) %reduce-scatter.25.cloned.1.call-update) | async-done | bytes 1552
  673.0 60.3 %reduce-scatter.17.cloned.1.call-done = bf16[128,768]{1,0:T(8,128)(2,1)} async-done(((bf16[1024,768]{1,0:T(8,128)(2,1)}), bf16[128,768]{1,0:T(8,128)(2,1)}) %reduce-scatter.17.cloned.1.call-update) | async-done | bytes 196624 | tf_op jit(solution)/shard_map/reduce_scatter | solution.py:269
  735.3 3.5 all-to-all-start.4
  740.6 4.9 all-to-all-done.4
  748.5 124.2 %reduce-scatter.19.cloned.1.call-done = bf16[32,1024]{1,0:T(8,128)(2,1)} async-done(((bf16[1024,1024]{1,0:T(8,128)(2,1)}), bf16[32,1024]{1,0:T(8,128)(2,1)}) %reduce-scatter.19.cloned.1.call-update) | async-done | bytes 65552 | tf_op jit(solution)/shard_map/reduce_scatter | solution.py:239
  (289 shorter events, 75.0 us)
Async XLA Ops:
  7.2 15.6 %copy-start.1 = (f32[2,64,1024]{2,1,0:T(8,128)S(1)}, f32[2,64,1024]{2,1,0:T(8,128)}, u32[]{:S(2)}) copy-start(f32[2,64,1024]{2,1,0:T(8,128)} %param.17) | copy-start | bytes 1572868
  7.2 66.2 %all-gather.8.cloned.1.call-start = ((), (), s32[]{:S(2)}) async-start(), calls=%async_computation.14 | async-start | bytes 3244032 | tf_op jit(solution)/shard_map/all_gather | solution.py:128
  11.2 107.9 %all-gather.12.cloned.1.call-start = ((), (), s32[]{:S(2)}) async-start(), calls=%async_computation.16 | async-start | bytes 1769472 | tf_op jit(solution)/shard_map/all_gather | solution.py:143
  22.7 113.6 %all-gather.10.cloned.1.call-start = ((), (), s32[]{:S(2)}) async-start(), calls=%async_computation.15 | async-start | bytes 1310720 | tf_op jit(solution)/shard_map/all_gather | solution.py:107
  77.3 110.7 %all-gather.16.cloned.1.call-start = ((), (), s32[]{:S(2)}) async-start(), calls=%async_computation.18 | async-start | bytes 2359296 | tf_op jit(solution)/shard_map/all_gather | solution.py:144
  142.3 9.4 %all-to-all-start.1 = ((bf16[2,256,256]{2,0,1:T(2,128)(2,1)}), bf16[2,256,256]{2,0,1:T(2,128)(2,1)S(1)}, u32[]{:S(2)}, u32[]{:S(2)}) async-start(bf16[2,256,256]{2,0,1:T(2,128)(2,1)} %copy.245), calls=%async_computation.1 | async-start | bytes 524288 | tf_op jit(solution)/shard_map/all_to_all | solution.py:181
  145.8 59.5 %all-gather.14.cloned.1.call-start = ((), (), s32[]{:S(2)}) async-start(), calls=%async_computation.17 | async-start | bytes 1310720 | tf_op jit(solution)/shard_map/all_gather | solution.py:107
  155.4 68.6 %all-gather.20.cloned.1.call-start = ((), (), s32[]{:S(2)}) async-start(), calls=%async_computation.21 | async-start | bytes 1310720 | tf_op jit(solution)/shard_map/all_gather | solution.py:107
  158.4 139.1 %reduce-scatter.23.cloned.1.call-start = ((), (), s32[]{:S(2)}) async-start(), calls=%async_computation.27 | async-start | bytes 2359296 | tf_op jit(solution)/shard_map/reduce_scatter | solution.py:215
  228.9 120.5 %all-gather.18.cloned.1.call-start = ((), (), s32[]{:S(2)}) async-start(), calls=%async_computation.19 | async-start | bytes 2359296 | tf_op jit(solution)/shard_map/all_gather | solution.py:145
  301.2 79.1 %reduce-scatter.13.cloned.1.call-start = ((), (), s32[]{:S(2)}) async-start(), calls=%async_computation.22 | async-start | bytes 1310720 | tf_op jit(solution)/shard_map/reduce_scatter | solution.py:111
  356.8 51.2 %reduce-scatter.11.cloned.1.call-start = ((), (), s32[]{:S(2)}) async-start(), calls=%async_computation.20 | async-start | bytes 1310720 | tf_op jit(solution)/shard_map/reduce_scatter | solution.py:111
  361.6 98.2 %reduce-scatter.15.cloned.1.call-start = ((), (), s32[]{:S(2)}) async-start(), calls=%async_computation.23 | async-start | bytes 1310720 | tf_op jit(solution)/shard_map/reduce_scatter | solution.py:111
  412.3 16.4 %copy-start.9 = (bf16[2,4,256,64]{2,3,1,0:T(8,128)(2,1)S(1)}, bf16[2,4,256,64]{2,3,1,0:T(8,128)(2,1)}, u32[]{:S(2)}) copy-start(bf16[2,4,256,64]{2,3,1,0:T(8,128)(2,1)} %copy-done.8) | copy-start | bytes 786436
  434.8 96.7 %reduce-scatter.21.cloned.1.call-start = ((), (), s32[]{:S(2)}) async-start(), calls=%async_computation.26 | async-start | bytes 2359296 | tf_op jit(solution)/shard_map/reduce_scatter | solution.py:219
  437.7 24.5 %copy-start.31 = (bf16[512,768]{0,1:T(8,128)(2,1)S(1)}, bf16[512,768]{0,1:T(8,128)(2,1)}, u32[]{:S(2)}) copy-start(bf16[512,768]{0,1:T(8,128)(2,1)} %copy-done.30) | copy-start | bytes 2359300
  437.7 230.8 %reduce-scatter.25.cloned.1.call-start = ((), (), s32[]{:S(2)}) async-start(), calls=%async_computation.28 | async-start | bytes 540672
  462.2 271.2 %reduce-scatter.17.cloned.1.call-start = ((), (), s32[]{:S(2)}) async-start(), calls=%async_computation.24 | async-start | bytes 1769472 | tf_op jit(solution)/shard_map/reduce_scatter | solution.py:269
  465.8 406.9 %reduce-scatter.19.cloned.1.call-start = ((), (), s32[]{:S(2)}) async-start(), calls=%async_computation.25 | async-start | bytes 2162688 | tf_op jit(solution)/shard_map/reduce_scatter | solution.py:239
  469.1 67.6 %copy-start.25 = (bf16[2,64,1024]{2,1,0:T(8,128)(2,1)S(1)}, bf16[2,64,1024]{2,1,0:T(8,128)(2,1)}, u32[]{:S(2)}) copy-start(bf16[2,64,1024]{2,1,0:T(8,128)(2,1)} %reduce-scatter.15.cloned.1.call-done) | copy-start | bytes 786436
  469.1 67.8 %copy-start.21 = (f32[128,1024]{1,0:T(8,128)S(1)}, f32[128,1024]{1,0:T(8,128)}, u32[]{:S(2)}) copy-start(f32[128,1024]{1,0:T(8,128)} %get-tuple-element.221) | copy-start | bytes 1572868
  533.1 9.5 %all-to-all-start.5 = ((bf16[128,8,1,128]{3,1,2,0:T(8,128)(2,1)}), bf16[128,8,1,128]{3,1,2,0:T(8,128)(2,1)S(1)}, u32[]{:S(2)}, u32[]{:S(2)}) async-start(bf16[128,8,1,128]{3,1,2,0:T(8,128)(2,1)} %bitcast.49), calls=%async_computation.11 | async-start | bytes 524288 | tf_op jit(solution)/shard_map/all_to_all | solution.py:68
  543.6 127.6 %copy-start.36 = (f32[5,32]{1,0:T(8,128)S(1)}, f32[5,32]{1,0:T(8,128)}, u32[]{:S(2)}) copy-start(f32[5,32]{1,0:T(8,128)} %param.22) | copy-start | bytes 1924
  543.7 128.2 %copy-start.40 = (f32[2,128]{1,0:T(2,128)S(1)}, f32[2,128]{1,0:T(2,128)}, u32[]{:S(2)}) copy-start(f32[2,128]{1,0:T(2,128)} %param.33) | copy-start | bytes 3076
  543.7 128.2 %copy-start.43 = (f32[128]{0:T(128)S(1)}, f32[128]{0:T(128)}, u32[]{:S(2)}) copy-start(f32[128]{0:T(128)} %param.26) | copy-start | bytes 1540
  543.7 128.8 %copy-start.38 = (f32[3,32]{1,0:T(4,128)S(1)}, f32[3,32]{1,0:T(4,128)}, u32[]{:S(2)}) copy-start(f32[3,32]{1,0:T(4,128)} %param.25) | copy-start | bytes 1156
  669.4 76.6 %copy-start.42 = (f32[128]{0:T(128)}, f32[128]{0:T(128)S(1)}, u32[]{:S(2)}) copy-start(f32[128]{0:T(128)S(1)} %reshape.514) | copy-start | bytes 1540
  670.4 76.0 %copy-start.35 = (f32[32,5]{0,1:T(8,128)}, f32[32,5]{0,1:T(8,128)S(1)}, u32[]{:S(2)}) copy-start(f32[32,5]{0,1:T(8,128)S(1)} %copy.292) | copy-start | bytes 1924
  671.2 75.1 %copy-start.37 = (f32[32,3]{0,1:T(4,128)}, f32[32,3]{0,1:T(4,128)S(1)}, u32[]{:S(2)}) copy-start(f32[32,3]{0,1:T(4,128)S(1)} %copy.293) | copy-start | bytes 1156
  735.3 10.2 %all-to-all-start.4 = ((bf16[128,3,1,256]{3,1,2,0:T(4,128)(2,1)}), bf16[128,3,1,256]{3,1,2,0:T(4,128)(2,1)S(1)}, u32[]{:S(2)}, u32[]{:S(2)}) async-start(bf16[128,3,1,256]{3,1,2,0:T(4,128)(2,1)} %copy.263), calls=%async_computation.8 | async-start | bytes 524288 | tf_op jit(solution)/shard_map/all_to_all | solution.py:68
  746.5 126.2 %copy-start.26 = (f32[2,32,1024]{2,1,0:T(8,128)S(1)}, f32[2,32,1024]{2,1,0:T(8,128)}, u32[]{:S(2)}) copy-start(f32[2,32,1024]{2,1,0:T(8,128)} %param.28) | copy-start | bytes 786436
  746.5 127.1 %copy-start.28 = (f32[32,1024]{1,0:T(8,128)S(1)}, f32[32,1024]{1,0:T(8,128)}, u32[]{:S(2)}) copy-start(f32[32,1024]{1,0:T(8,128)} %param.21) | copy-start | bytes 393220
  (36 other events, 98.6 us)
Sparse Core Ops, SparseCore 0:
  11.5 61.8 all-gather.7
  76.2 42.8 all-gather.11
  121.2 15.0 all-gather.9
  138.9 49.0 all-gather.15
  190.0 15.2 all-gather.13
  207.3 16.6 all-gather.19
  229.1 68.4 reduce-scatter.22
  301.3 48.1 all-gather.17
  356.9 23.2 reduce-scatter.12
  383.2 24.7 reduce-scatter.10
  434.9 24.8 reduce-scatter.14
  463.1 68.2 reduce-scatter.20
  533.7 134.8 reduce-scatter.24
  671.8 61.4 reduce-scatter.16
  735.4 137.2 reduce-scatter.18
where the time goes:
time: 883 us; the launch traced here: 882 us
  waiting for transfers between devices  723 us (82%)
  matrix products  40.4 us (5%)
  local copies, waits for them, and re-layouts  33.8 us (4%)
  other arithmetic  31 us (4%)
  blocking collectives  27 us (3%)
  between operations  15 us (2%)
  starting transfers between devices  11.4 us (1%)
    reduce_scatter x1, waiting for transfers between devices, body(): lax.psum_scatter(outer(attended, middle_half), whole, scatter_dimension=0...  124 us
    unnamed x16, waiting for transfers between devices  123 us
    reduce_scatter x1, waiting for transfers between devices, body(): lax.psum_scatter(outer(active, cot_all), 'dp', scatter_dimension=0, tiled...  68.5 us
    reduce_scatter x3, waiting for transfers between devices, scatter_rows(): lax.psum_scatter(halved(partial).reshape(slot_count, length, -1), 'seq',...  64.8 us
    reduce_scatter x1, waiting for transfers between devices, body(): lax.psum_scatter(outer(lifted_two, upper_half), 'dp', scatter_dimension=0...  62.3 us
    reduce_scatter x1, waiting for transfers between devices, body(): lax.psum_scatter(outer(lifted_one, packed_grad), 'dp', scatter_dimension=...  60.3 us
    all_gather x1, waiting for transfers between devices, body(): lax.all_gather(jnp.concatenate([halved(outward), small_block], axis=0), w...  50.3 us
    all_gather x3, waiting for transfers between devices, gather_rows(): lax.all_gather(local.reshape(slot_count, block_size, -1), 'seq', axis=1,...  48.7 us
  transfers between devices with their start and end apart: 18, of which 18 were waited for; matrix products, arithmetic and copies ran while one was open for 7% of the time, Pallas kernels for 0%

commit v1 on v0

--- a/solution.py
+++ b/solution.py
@@ -104,7 +104,32 @@
     whole = ("dp", "seq")
 
     def gather_rows(local):
-        full = lax.all_gather(local.reshape(slot_count, block_size, -1), "seq", axis=1, tiled=True)
+
+        def _view_trails(own_rows):
+            local_out = lax.axis_index("seq")
+            current_arr = lax.axis_size("seq")
+            local_part, work_now, back = (current_arr, local_out, own_rows.shape[1])
+            frames = [(dev_j, (dev_j + 1) % local_part) for dev_j in range(local_part)]
+            bank = [(dev_j, (dev_j - 1) % local_part) for dev_j in range(local_part)]
+            wide_out = jnp.zeros(
+                (*own_rows.shape[:1], local_part * back, *own_rows.shape[2:]), own_rows.dtype
+            )
+            wide_out = lax.dynamic_update_slice_in_dim(wide_out, own_rows, work_now * back, axis=1)
+            p_next = seen_now = own_rows
+            passed = local_part // 2
+            for k0 in [*range(1, passed + 1)]:
+                p_next = lax.ppermute(p_next, "seq", frames)
+                wide_out = lax.dynamic_update_slice_in_dim(
+                    wide_out, p_next, (work_now - k0) % local_part * back, axis=1
+                )
+                if k0 < local_part - passed:
+                    seen_now = lax.ppermute(seen_now, "seq", bank)
+                    wide_out = lax.dynamic_update_slice_in_dim(
+                        wide_out, seen_now, (work_now + k0) % local_part * back, axis=1
+                    )
+            return wide_out
+
+        full = _view_trails(local.reshape(slot_count, block_size, -1))
         return full.reshape(all_rows, -1)
 
     def scatter_rows(partial):

time: 883 us -> 830 us (0.940)
  waiting for transfers between devices: 723 us -> 662 us
  local copies, waits for them, and re-layouts: 33.8 us -> 45.2 us
  starting transfers between devices: 11.4 us -> 20.4 us
    all_gather x3 -> x0, waiting for transfers between devices: 48.7 us -> none  [gather_rows(): lax.all_gather(local.reshape(slot_count, block_size, -1), 'seq', axis=1,...]
    ppermute x0 -> x9, waiting for transfers between devices: none -> 14.1 us  [the longest x6 10.8 us: _view_trails(): p_next = lax.ppermute(p_next, 'seq', frames)]
    all_gather x1, waiting for transfers between devices: 29.5 us -> 16.2 us  [body(): up_part = lax.all_gather(moved_up, 'dp', axis=0, tiled=True)]
    all_to_all x2 -> x1, blocking collectives: 17.9 us -> 9.5 us  [spread_columns(): moved = lax.all_to_all(parts, 'seq', 2, 0, tiled=True)]
    unnamed x16 -> x13, waiting for transfers between devices: 123 us -> 123 us
  transfers between devices with their start and end apart: 18 -> 25, of which waited for: 18 -> 20; matrix products, arithmetic and copies ran while one was open for 7% -> 8% of each run, Pallas kernels for 0% -> 0%
where the time goes in v1:
time: 830 us; the launch traced here: 828 us
  waiting for transfers between devices  662 us (80%)
  local copies, waits for them, and re-layouts  45.2 us (5%)
  matrix products  38.4 us (5%)
  other arithmetic  28.6 us (3%)
  starting transfers between devices  20.4 us (2%)
  blocking collectives  18.6 us (2%)
  between operations  15.4 us (2%)
    reduce_scatter x1, waiting for transfers between devices, body(): lax.psum_scatter(outer(attended, middle_half), whole, scatter_dimension=0...  124 us
    unnamed x13, waiting for transfers between devices  123 us
    reduce_scatter x1, waiting for transfers between devices, body(): lax.psum_scatter(outer(active, cot_all), 'dp', scatter_dimension=0, tiled...  66.8 us
    reduce_scatter x3, waiting for transfers between devices, scatter_rows(): lax.psum_scatter(halved(partial).reshape(slot_count, length, -1), 'seq',...  63.5 us
    reduce_scatter x1, waiting for transfers between devices, body(): lax.psum_scatter(outer(lifted_two, upper_half), 'dp', scatter_dimension=0...  62.7 us
    reduce_scatter x1, waiting for transfers between devices, body(): lax.psum_scatter(outer(lifted_one, packed_grad), 'dp', scatter_dimension=...  60.6 us
    all_gather x1, waiting for transfers between devices, body(): down_part = lax.all_gather(halved(shrink), 'dp', axis=0, tiled=True)  48.2 us
    all_gather x1, waiting for transfers between devices, body(): lax.all_gather(jnp.concatenate([halved(outward), small_block], axis=0), w...  45.6 us
  transfers between devices with their start and end apart: 25, of which 20 were waited for; matrix products, arithmetic and copies ran while one was open for 8% of the time, Pallas kernels for 0%

profile of v1, /device:TPU:0, one launch (start us, length us, event | category | flops | bytes accessed | tf_op | source)
XLA Modules:
  0.0 828.2 jit_solution(13371358602193558532)
XLA Ops:
  12.5 9.5 %all_to_all.78 = bf16[32,3,4,256]{3,0,1,2:T(8,128)(2,1)S(1)} all-to-all(bf16[32,3,4,256]{3,0,1,2:T(8,128)(2,1)S(1)} %copy.236), channel_id=1, replica_groups=mesh['dp'=8,'seq'=4] {'seq'}, dimensions={2} | all-to-all | bytes 393216 | tf_op jit(solution)/shard_map/all_to_all | solution.py:61
  23.8 3.4 all-to-all-start.2
  27.9 45.6 %all-gather.5.cloned.1.call-done = bf16[1536,1024]{1,0:T(8,128)(2,1)} async-done(((bf16[48,1024]{1,0:T(8,128)(2,1)}), bf16[1536,1024]{1,0:T(8,128)(2,1)}) %all-gather.5.cloned.1.call-update) | async-done | bytes 3145744 | tf_op jit(solution)/shard_map/all_gather | solution.py:153
  81.1 2.4 collective-permute-done
  85.5 5.5 collective-permute-done.2
  91.1 28.1 %all-gather.7.cloned.1.call-done = bf16[1024,768]{1,0:T(8,128)(2,1)} async-done(((bf16[128,768]{1,0:T(8,128)(2,1)}), bf16[1024,768]{1,0:T(8,128)(2,1)}) %all-gather.7.cloned.1.call-update) | async-done | bytes 1572880 | tf_op jit(solution)/shard_map/all_gather | solution.py:168
  119.1 2.7 fusion.89
  125.1 3.4 all-to-all-start.1
  131.9 3.3 slice.165
  146.8 2.5 collective-permute-done.4
  153.1 16.2 %all-gather.9.cloned.1.call-done = bf16[1024,1024]{1,0:T(8,128)(2,1)} async-done(((bf16[128,1024]{1,0:T(8,128)(2,1)}), bf16[1024,1024]{1,0:T(8,128)(2,1)}) %all-gather.9.cloned.1.call-update) | async-done | bytes 2097168 | tf_op jit(solution)/shard_map/all_gather | solution.py:169
  169.3 3.2 fusion.90
  173.9 3.1 convolution_convert_fusion
  177.3 66.8 %reduce-scatter.23.cloned.1.call-done = bf16[128,1024]{1,0:T(8,128)(2,1)} async-done(((bf16[1024,1024]{1,0:T(8,128)(2,1)}), bf16[128,1024]{1,0:T(8,128)(2,1)}) %reduce-scatter.23.cloned.1.call-update) | async-done | bytes 262160 | tf_op jit(solution)/shard_map/reduce_scatter | solution.py:240
  247.7 48.2 %all-gather.11.cloned.1.call-done = bf16[1024,1024]{1,0:T(8,128)(2,1)} async-done(((bf16[128,1024]{1,0:T(8,128)(2,1)}), bf16[1024,1024]{1,0:T(8,128)(2,1)}) %all-gather.11.cloned.1.call-update) | async-done | bytes 2097168 | tf_op jit(solution)/shard_map/all_gather | solution.py:170
  295.9 5.1 fusion.88
  303.4 4.7 convolution_convert_fusion.6
  308.2 18.6 %reduce-scatter.13.cloned.1.call-done = bf16[2,64,1024]{2,1,0:T(8,128)(2,1)} async-done(((bf16[2,256,1024]{2,1,0:T(8,128)(2,1)}), bf16[2,64,1024]{2,1,0:T(8,128)(2,1)}) %reduce-scatter.13.cloned.1.call-update) | async-done | bytes 262160 | tf_op jit(solution)/shard_map/reduce_scatter | solution.py:136
  329.3 24.9 %reduce-scatter.11.cloned.1.call-done = bf16[2,64,1024]{2,1,0:T(8,128)(2,1)} async-done(((bf16[2,256,1024]{2,1,0:T(8,128)(2,1)}), bf16[2,64,1024]{2,1,0:T(8,128)(2,1)}) %reduce-scatter.11.cloned.1.call-update) | async-done | bytes 262160 | tf_op jit(solution)/shard_map/reduce_scatter | solution.py:136
  354.2 2.4 fusion.81
  360.0 9.1 %all_to_all.79 = bf16[4,2,16384]{2,1,0:T(2,128)(2,1)} all-to-all(bf16[4,2,16384]{2,1,0:T(2,128)(2,1)S(1)} %reshape.573), channel_id=1, replica_groups=mesh['dp'=8,'seq'=4] {'seq'}, dimensions={0} | all-to-all | bytes 524288 | tf_op jit(solution)/shard_map/all_to_all | solution.py:260
  381.0 3.8 convolution_convert_fusion.1
  385.9 20.0 %reduce-scatter.15.cloned.1.call-done = bf16[2,64,1024]{2,1,0:T(8,128)(2,1)} async-done(((bf16[2,256,1024]{2,1,0:T(8,128)(2,1)}), bf16[2,64,1024]{2,1,0:T(8,128)(2,1)}) %reduce-scatter.15.cloned.1.call-update) | async-done | bytes 262160 | tf_op jit(solution)/shard_map/reduce_scatter | solution.py:136
  408.4 3.4 convolution_convert_fusion.3
  415.3 62.7 %reduce-scatter.21.cloned.1.call-done = bf16[128,1024]{1,0:T(8,128)(2,1)} async-done(((bf16[1024,1024]{1,0:T(8,128)(2,1)}), bf16[128,1024]{1,0:T(8,128)(2,1)}) %reduce-scatter.21.cloned.1.call-update) | async-done | bytes 262160 | tf_op jit(solution)/shard_map/reduce_scatter | solution.py:244
  479.6 3.4 all-to-all-start.5
  484.6 4.5 all-to-all-done.5
  492.4 122.4 %reduce-scatter.25.cloned.1.call-done = f32[32,12]{1,0:T(8,128)} async-done(((f32[1024,12]{1,0:T(8,128)}), f32[32,12]{1,0:T(8,128)}) %reduce-scatter.25.cloned.1.call-update) | async-done | bytes 1552
  619.3 60.6 %reduce-scatter.17.cloned.1.call-done = bf16[128,768]{1,0:T(8,128)(2,1)} async-done(((bf16[1024,768]{1,0:T(8,128)(2,1)}), bf16[128,768]{1,0:T(8,128)(2,1)}) %reduce-scatter.17.cloned.1.call-update) | async-done | bytes 196624 | tf_op jit(solution)/shard_map/reduce_scatter | solution.py:294
  681.9 3.5 all-to-all-start.4
  687.2 4.9 all-to-all-done.4
  695.1 123.8 %reduce-scatter.19.cloned.1.call-done = bf16[32,1024]{1,0:T(8,128)(2,1)} async-done(((bf16[1024,1024]{1,0:T(8,128)(2,1)}), bf16[32,1024]{1,0:T(8,128)(2,1)}) %reduce-scatter.19.cloned.1.call-update) | async-done | bytes 65552 | tf_op jit(solution)/shard_map/reduce_scatter | solution.py:264
  (324 shorter events, 91.1 us)
Async XLA Ops:
  7.2 66.2 %all-gather.5.cloned.1.call-start = ((), (), s32[]{:S(2)}) async-start(), calls=%async_computation.14 | async-start | bytes 3244032 | tf_op jit(solution)/shard_map/all_gather | solution.py:153
  11.2 107.9 %all-gather.7.cloned.1.call-start = ((), (), s32[]{:S(2)}) async-start(), calls=%async_computation.15 | async-start | bytes 1769472 | tf_op jit(solution)/shard_map/all_gather | solution.py:168
  23.8 59.7 %all-to-all-start.2 = ((bf16[32,8,4,128]{3,1,0,2:T(8,128)(2,1)}), bf16[32,8,4,128]{3,1,0,2:T(8,128)(2,1)S(1)}, u32[]{:S(2)}, u32[]{:S(2)}) async-start(bf16[32,8,4,128]{3,1,0,2:T(8,128)(2,1)} %copy.248), calls=%async_computation.2 | async-start | bytes 524288 | tf_op jit(solution)/shard_map/all_to_all | solution.py:61
  27.2 142.1 %all-gather.9.cloned.1.call-start = ((), (), s32[]{:S(2)}) async-start(), calls=%async_computation.16 | async-start | bytes 2359296 | tf_op jit(solution)/shard_map/all_gather | solution.py:169
  76.7 6.7 collective-permute-start
  77.2 8.3 collective-permute-start.1
  80.6 49.6 %collective-permute-start.6 = (bf16[2,64,1024]{2,1,0:T(8,128)(2,1)}, bf16[2,64,1024]{2,1,0:T(8,128)(2,1)}, u32[]{:S(2)}, u32[]{:S(2)}) collective-permute-start(bf16[2,64,1024]{2,1,0:T(8,128)(2,1)} %get-tuple-element.209), channel_id=1, source_target_pairs={{0,1},{1,2},{2,3},{3,0},{4,5},{5,6},{6,7},{7,4},{8,9},{9,10},{10,1... | collective-permute-start | bytes 786440 | tf_op jit(solution)/shard_map/ppermute | solution.py:121
  83.4 7.6 collective-permute-start.2
  125.1 10.3 %all-to-all-start.1 = ((bf16[2,256,256]{2,0,1:T(2,128)(2,1)}), bf16[2,256,256]{2,0,1:T(2,128)(2,1)S(1)}, u32[]{:S(2)}, u32[]{:S(2)}) async-start(bf16[2,256,256]{2,0,1:T(2,128)(2,1)} %copy.245), calls=%async_computation.1 | async-start | bytes 524288 | tf_op jit(solution)/shard_map/all_to_all | solution.py:206
  128.5 115.5 %reduce-scatter.23.cloned.1.call-start = ((), (), s32[]{:S(2)}) async-start(), calls=%async_computation.24 | async-start | bytes 2359296 | tf_op jit(solution)/shard_map/reduce_scatter | solution.py:240
  128.6 10.4 %collective-permute-start.7 = (bf16[2,64,1024]{2,1,0:T(8,128)(2,1)}, bf16[2,64,1024]{2,1,0:T(8,128)(2,1)}, u32[]{:S(2)}, u32[]{:S(2)}) collective-permute-start(bf16[2,64,1024]{2,1,0:T(8,128)(2,1)} %get-tuple-element.209), channel_id=1, source_target_pairs={{0,3},{1,0},{2,1},{3,2},{4,7},{5,4},{6,5},{7,6},{8,11},{9,8},{10,9... | collective-permute-start | bytes 786440 | tf_op jit(solution)/shard_map/ppermute | solution.py:126
  130.3 10.4 %collective-permute-start.8 = (bf16[2,64,1024]{2,1,0:T(8,128)(2,1)}, bf16[2,64,1024]{2,1,0:T(8,128)(2,1)}, u32[]{:S(2)}, u32[]{:S(2)}) collective-permute-start(bf16[2,64,1024]{2,1,0:T(8,128)(2,1)} %collective-permute-done.6), channel_id=1, source_target_pairs={{0,1},{1,2},{2,3},{3,0},{4,5},{5,6},{6,7},{7,4},{8,9},{9,10},{10,1... | collective-permute-start | bytes 786440 | tf_op jit(solution)/shard_map/ppermute | solution.py:121
  138.4 5.9 collective-permute-start.3
  142.3 7.0 collective-permute-start.4
  144.3 8.1 collective-permute-start.5
  177.0 118.9 %all-gather.11.cloned.1.call-start = ((), (), s32[]{:S(2)}) async-start(), calls=%async_computation.17 | async-start | bytes 2359296 | tf_op jit(solution)/shard_map/all_gather | solution.py:170
  247.7 79.2 %reduce-scatter.13.cloned.1.call-start = ((), (), s32[]{:S(2)}) async-start(), calls=%async_computation.19 | async-start | bytes 1310720 | tf_op jit(solution)/shard_map/reduce_scatter | solution.py:136
  303.3 50.8 %reduce-scatter.11.cloned.1.call-start = ((), (), s32[]{:S(2)}) async-start(), calls=%async_computation.18 | async-start | bytes 1310720 | tf_op jit(solution)/shard_map/reduce_scatter | solution.py:136
  308.1 97.8 %reduce-scatter.15.cloned.1.call-start = ((), (), s32[]{:S(2)}) async-start(), calls=%async_computation.20 | async-start | bytes 1310720 | tf_op jit(solution)/shard_map/reduce_scatter | solution.py:136
  381.0 97.0 %reduce-scatter.21.cloned.1.call-start = ((), (), s32[]{:S(2)}) async-start(), calls=%async_computation.23 | async-start | bytes 2359296 | tf_op jit(solution)/shard_map/reduce_scatter | solution.py:244
  384.9 230.0 %reduce-scatter.25.cloned.1.call-start = ((), (), s32[]{:S(2)}) async-start(), calls=%async_computation.25 | async-start | bytes 540672
  408.4 271.6 %reduce-scatter.17.cloned.1.call-start = ((), (), s32[]{:S(2)}) async-start(), calls=%async_computation.21 | async-start | bytes 1769472 | tf_op jit(solution)/shard_map/reduce_scatter | solution.py:294
  411.9 407.1 %reduce-scatter.19.cloned.1.call-start = ((), (), s32[]{:S(2)}) async-start(), calls=%async_computation.22 | async-start | bytes 2162688 | tf_op jit(solution)/shard_map/reduce_scatter | solution.py:264
  479.6 9.5 %all-to-all-start.5 = ((bf16[128,8,1,128]{3,1,2,0:T(8,128)(2,1)}), bf16[128,8,1,128]{3,1,2,0:T(8,128)(2,1)S(1)}, u32[]{:S(2)}, u32[]{:S(2)}) async-start(bf16[128,8,1,128]{3,1,2,0:T(8,128)(2,1)} %bitcast.49), calls=%async_computation.11 | async-start | bytes 524288 | tf_op jit(solution)/shard_map/all_to_all | solution.py:68
  490.1 127.4 %copy-start.40 = (f32[5,32]{1,0:T(8,128)S(1)}, f32[5,32]{1,0:T(8,128)}, u32[]{:S(2)}) copy-start(f32[5,32]{1,0:T(8,128)} %param.22) | copy-start | bytes 1924
  490.2 128.0 %copy-start.44 = (f32[2,128]{1,0:T(2,128)S(1)}, f32[2,128]{1,0:T(2,128)}, u32[]{:S(2)}) copy-start(f32[2,128]{1,0:T(2,128)} %param.33) | copy-start | bytes 3076
  490.2 128.0 %copy-start.49 = (f32[128]{0:T(128)S(1)}, f32[128]{0:T(128)}, u32[]{:S(2)}) copy-start(f32[128]{0:T(128)} %param.26) | copy-start | bytes 1540
  490.2 128.5 %copy-start.42 = (f32[3,32]{1,0:T(4,128)S(1)}, f32[3,32]{1,0:T(4,128)}, u32[]{:S(2)}) copy-start(f32[3,32]{1,0:T(4,128)} %param.25) | copy-start | bytes 1156
  615.8 77.0 %copy-start.48 = (f32[128]{0:T(128)}, f32[128]{0:T(128)S(1)}, u32[]{:S(2)}) copy-start(f32[128]{0:T(128)S(1)} %reshape.514) | copy-start | bytes 1540
  681.9 10.2 %all-to-all-start.4 = ((bf16[128,3,1,256]{3,1,2,0:T(4,128)(2,1)}), bf16[128,3,1,256]{3,1,2,0:T(4,128)(2,1)S(1)}, u32[]{:S(2)}, u32[]{:S(2)}) async-start(bf16[128,3,1,256]{3,1,2,0:T(4,128)(2,1)} %copy.263), calls=%async_computation.8 | async-start | bytes 524288 | tf_op jit(solution)/shard_map/all_to_all | solution.py:68
  693.1 125.8 %copy-start.30 = (f32[2,32,1024]{2,1,0:T(8,128)S(1)}, f32[2,32,1024]{2,1,0:T(8,128)}, u32[]{:S(2)}) copy-start(f32[2,32,1024]{2,1,0:T(8,128)} %param.28) | copy-start | bytes 786436
  693.1 126.7 %copy-start.33 = (f32[32,1024]{1,0:T(8,128)S(1)}, f32[32,1024]{1,0:T(8,128)}, u32[]{:S(2)}) copy-start(f32[32,1024]{1,0:T(8,128)} %param.21) | copy-start | bytes 393220
  (49 other events, 621.3 us)
Sparse Core Ops, SparseCore 0:
  11.5 61.8 all-gather.4
  76.2 42.8 all-gather.6
  121.8 47.4 all-gather.8
  177.1 66.8 reduce-scatter.22
  247.8 48.1 all-gather.10
  303.5 23.3 reduce-scatter.12
  329.4 24.7 reduce-scatter.10
  381.1 24.8 reduce-scatter.14
  409.5 68.4 reduce-scatter.20
  480.0 134.7 reduce-scatter.24
  618.3 61.6 reduce-scatter.16
  682.1 136.8 reduce-scatter.18
